TPU v7x, 128 devices: a whole 4x4x4 slice. The times are simulated.
128 devices in a mesh: frame: 16 (over y, x), head: 8 (over z, core).
Axes of the slice: x: 4, y: 4, z: 4, core: 2. Of those that a mesh axis runs over, the one named last changes fastest.
Arguments:
- tokens: bfloat16 [12288, 5120], P('frame', 'head'), may hold values from -40 to 40
- mask_block_frame: int32 [96], replicated, may hold values from 0 to 7, as said below
- attended_key_blocks: int32 [96, 10], replicated, may hold values from 0 to 95, as said below
- frozen_query_key_value: bfloat16 [5120, 3, 3072], P(None, None, 'head'), may hold values from -0.104815686 to 0.104815686
- query_key_value_down_weight: bfloat16 [5120, 192], replicated, may hold values from -0.078125 to 0.078125
- query_key_value_up_weight: bfloat16 [64, 3, 3072], P(None, None, 'head'), may hold values from -0.375 to 0.375
- frozen_output_weight: bfloat16 [3072, 5120], P('head'), may hold values from -0.109375 to 0.109375
- output_down_weight: bfloat16 [3072, 64], P('head'), may hold values from -0.109375 to 0.109375
- output_up_weight: bfloat16 [64, 5120], P(None, 'head'), may hold values from -0.75 to 0.75
Outputs:
- attended_out: bfloat16 [12288, 5120], P('frame', 'head')
Inputs may be any that keep to these rules, and one draw needn't show every extreme that they name: `mask_block_frame`: Non-decreasing along the blocks; every frame from 0 to 7 holds at least one block. `attended_key_blocks`: row b lists 10 distinct key blocks and always includes b itself. Take aligned groups of 6 blocks; for a group of query blocks and another group g groups away (g >= 1), the rows of the first group together name exactly 4 // 2 ** (g - 1) distinct blocks of the second, except that a group exactly 8 groups away is named by exactly the larger of that number and 2.
All inputs are finite; a program needn't handle non-finite values.
Results may differ from a plain program's by a relative error of at most 0.017.
Values may be sent and summed in bfloat16 or wider, within the bound.
A program may use at most 128 MiB of HBM per device.

v0:
```python
import math
import jax
import jax.numpy as jnp
from jax import lax
from jax.sharding import PartitionSpec as P

MODEL_WIDTH = 5120
HEAD_SIZE = 128
BLOCK = 128


def rotate_pairs(values, frame_pos, place):
    time_pairs = (HEAD_SIZE - 4 * (HEAD_SIZE // 6)) // 2
    space_pairs = (HEAD_SIZE - 2 * time_pairs) // 2
    time_freq = 10000.0 ** (-jnp.arange(time_pairs).astype(jnp.float32) / time_pairs)
    space_freq = 10000.0 ** (-jnp.arange(space_pairs).astype(jnp.float32) / space_pairs)
    time_angle = frame_pos[:, None] * time_freq[None, :]
    space_angle = place[:, None] * space_freq[None, :]
    cos_time = jnp.cos(time_angle)[:, None, :]
    sin_time = jnp.sin(time_angle)[:, None, :]
    cos_space = jnp.cos(space_angle)[:, None, :]
    sin_space = jnp.sin(space_angle)[:, None, :]
    first_part = values[:, :, :time_pairs]
    second_part = values[:, :, time_pairs : 2 * time_pairs]
    third_part = values[:, :, 2 * time_pairs : 2 * time_pairs + space_pairs]
    fourth_part = values[:, :, 2 * time_pairs + space_pairs :]
    return jnp.concatenate(
        [
            first_part * cos_time - second_part * sin_time,
            first_part * sin_time + second_part * cos_time,
            third_part * cos_space - fourth_part * sin_space,
            third_part * sin_space + fourth_part * cos_space,
        ],
        axis=-1,
    )


def token_positions(mask_block_frame, block_ids):
    count_blocks = mask_block_frame.shape[0]
    all_blocks = jnp.arange(count_blocks)
    same_frame = mask_block_frame[:, None] == mask_block_frame[None, :]
    first_block = jnp.min(jnp.where(same_frame, all_blocks[None, :], count_blocks), axis=1)
    inner_ids = jnp.arange(BLOCK)
    token_ids = block_ids[:, None] * BLOCK + inner_ids[None, :]
    frame_pos = (
        jnp.broadcast_to(mask_block_frame[block_ids][:, None], token_ids.shape)
        .reshape(-1)
        .astype(jnp.float32)
    )
    place = (token_ids - first_block[block_ids][:, None] * BLOCK).reshape(-1).astype(jnp.float32)
    return (frame_pos, place)


def body(
    tokens,
    mask_block_frame,
    attended_key_blocks,
    frozen_query_key_value,
    query_key_value_down_weight,
    query_key_value_up_weight,
    frozen_output_weight,
    output_down_weight,
    output_up_weight,
):
    tok_rows = tokens.shape[0]
    blocks_here = tok_rows // BLOCK
    local_width = frozen_output_weight.shape[0]
    heads_here = local_width // HEAD_SIZE
    adapter_rank_width = output_up_weight.shape[0]
    listed = attended_key_blocks.shape[1]
    weights_flat = frozen_query_key_value.reshape(MODEL_WIDTH, 3 * local_width)
    rank_segment = lax.all_gather(tokens, "head", axis=1, tiled=True)
    projected_rows = jnp.dot(rank_segment, weights_flat, preferred_element_type=jnp.float32)
    adapter_output_sum = jnp.dot(
        rank_segment, query_key_value_down_weight, preferred_element_type=jnp.float32
    )
    adapter_query_key_value = adapter_output_sum.astype(jnp.bfloat16).reshape(
        tok_rows, 3, adapter_rank_width
    )
    projected_rows = projected_rows.reshape(tok_rows, 3, local_width) + jnp.einsum(
        "ngc,cgz->ngz",
        adapter_query_key_value,
        query_key_value_up_weight,
        preferred_element_type=jnp.float32,
    )
    frame_index = lax.axis_index("frame")
    block_ids = frame_index * blocks_here + jnp.arange(blocks_here, dtype=jnp.int32)
    frame_pos, place = token_positions(mask_block_frame, block_ids)
    queries = rotate_pairs(
        projected_rows[:, 0].reshape(tok_rows, heads_here, HEAD_SIZE), frame_pos, place
    ).astype(jnp.bfloat16)
    keys = rotate_pairs(
        projected_rows[:, 1].reshape(tok_rows, heads_here, HEAD_SIZE), frame_pos, place
    ).astype(jnp.bfloat16)
    key_tiles = keys.reshape(blocks_here, BLOCK, local_width)
    value_tiles = projected_rows[:, 2].astype(jnp.bfloat16).reshape(blocks_here, BLOCK, local_width)
    my_lists = lax.dynamic_slice_in_dim(
        attended_key_blocks, frame_index * blocks_here, blocks_here, 0
    )
    pool_keys, pool_values = (
        lax.all_gather(key_tiles, "frame", axis=0, tiled=True),
        lax.all_gather(value_tiles, "frame", axis=0, tiled=True),
    )
    chosen_keys = pool_keys[my_lists].reshape(blocks_here, listed * BLOCK, heads_here, HEAD_SIZE)
    chosen_values = pool_values[my_lists].reshape(
        blocks_here, listed * BLOCK, heads_here, HEAD_SIZE
    )
    query_tiles = queries.reshape(blocks_here, BLOCK, heads_here, HEAD_SIZE)
    scores = jnp.einsum(
        "nqhd,nkhd->nhqk", query_tiles, chosen_keys, preferred_element_type=jnp.float32
    ) / math.sqrt(HEAD_SIZE)
    row_max = jnp.max(scores, axis=-1, keepdims=True)
    powers = jnp.exp(scores - row_max)
    probs = (powers / jnp.sum(powers, axis=-1, keepdims=True)).astype(jnp.bfloat16)
    attention_result = jnp.einsum(
        "nhqk,nkhd->nqhd", probs, chosen_values, preferred_element_type=jnp.float32
    ).astype(jnp.bfloat16)
    attention_result = attention_result.reshape(tok_rows, local_width)
    adapter_output = lax.psum(
        jnp.dot(attention_result, output_down_weight, preferred_element_type=jnp.float32).astype(
            jnp.bfloat16
        ),
        "head",
    )
    partial_value = jnp.dot(
        attention_result, frozen_output_weight, preferred_element_type=jnp.float32
    )
    frozen_output = lax.psum_scatter(
        partial_value.astype(jnp.bfloat16), "head", scatter_dimension=1, tiled=True
    ).astype(jnp.float32)
    return (
        frozen_output
        + jnp.dot(adapter_output, output_up_weight, preferred_element_type=jnp.float32)
    ).astype(jnp.bfloat16)


def solution(mesh):
    return jax.shard_map(
        body,
        mesh=mesh,
        in_specs=(
            P("frame", "head"),
            P(),
            P(),
            P(None, None, "head"),
            P(),
            P(None, None, "head"),
            P("head", None),
            P("head", None),
            P(None, "head"),
        ),
        out_specs=P("frame", "head"),
        check_vma=False,
    )
```

profile of v0, /device:TPU:0, one launch (start us, length us, event | category | flops | bytes accessed | tf_op | source)
XLA Modules:
  0.0 407.3 jit_solution(18228735309528296065)
XLA Ops:
  6.5 0.7 all-gather.4.cloned.1.call-update
  7.3 1.3 gather_fusion.1
  8.6 0.9 select_reduce_fusion
  9.6 0.6 gather_fusion.2
  10.2 16.2 %copy.37 = bf16[5120,3,384]{0,2,1:T(8,128)(2,1)} copy(bf16[5120,3,384]{2,0,1:T(8,128)(2,1)} %param.12) | data formatting | bytes 23592960 | tf_op args[3]
  26.6 0.3 multiply_cosine_fusion.1
  26.9 0.6 multiply_cosine_fusion
  27.5 31.6 %all-gather.4.cloned.1.call-done = bf16[768,5120]{1,0:T(8,128)(2,1)} async-done(((bf16[768,640]{1,0:T(8,128)(2,1)}), bf16[768,5120]{1,0:T(8,128)(2,1)}) %all-gather.4.cloned.1.call-update) | async-done | bytes 7864336 | tf_op jit(solution)/shard_map/all_gather | solution.py:72
  59.2 6.1 %convolution_convert_fusion.1 = bf16[768,192]{0,1:T(8,128)(2,1)S(1)} fusion(bf16[768,5120]{1,0:T(8,128)(2,1)} %all-gather.4.cloned.1.call-done, bf16[5120,192]{0,1:T(8,128)(2,1)S(1)} %copy-done), kind=kOutput, calls=%fused_computation.22 | convolution fusion | flops 1510096896 | bytes 10125312 | tf_op jit(solution)/shard_map/dot_general | solution.py:74
  65.3 0.7 fusion.38
  66.0 13.3 %bitcast_add_fusion = f32[768,3,384]{0,2,1:T(8,128)S(1)} fusion(f32[3,768,384]{1,2,0:T(8,128)S(1)} %fusion.38, bf16[5120,3,384]{0,2,1:T(8,128)(2,1)S(1)} %copy-done.2, bf16[768,5120]{1,0:T(8,128)(2,1)} %all-gather.4.cloned.1.call-done), kind=kOutput, calls=%fused_computation.18 | convolution fusion | flops 9060581376 | bytes 26738688 | tf_op jit(solution)/shard_map/dot_general | solution.py:73
  79.3 0.2 fusion.36
  79.5 0.3 subtract_convert_fusion.1
  79.8 0.1 subtract_convert_fusion.3
  80.0 1.1 copy-done.3
  81.0 0.2 pad_maximum_fusion
  81.2 0.7 convert_element_type.81
  81.9 1.3 copy.45
  83.2 1.3 slice.81
  84.5 1.1 copy.38
  85.6 0.2 reduce-scatter.4.cloned.1.call-start
  85.9 0.1 copy.39
  86.1 0.2 concatenate.19
  86.4 0.4 copy.43
  86.8 0.2 concatenate.20
  87.0 0.4 copy.44
  87.5 0.1 concatenate.17
  87.6 0.4 copy.41
  88.0 0.1 concatenate.18
  88.1 0.4 copy.42
  88.5 70.3 %all-gather.8.cloned.1.call-done = bf16[96,128,384]{2,1,0:T(8,128)(2,1)} async-done(((bf16[6,128,384]{2,1,0:T(8,128)(2,1)}), bf16[96,128,384]{2,1,0:T(8,128)(2,1)}) %all-gather.8.cloned.1.call-update) | async-done | bytes 9437200 | tf_op jit(solution)/shard_map/all_gather | solution.py:101
  158.8 7.7 %gather_fusion.3 = bf16[60,128,384]{2,1,0:T(8,128)(2,1)} fusion(bf16[96,128,384]{2,1,0:T(8,128)(2,1)} %all-gather.8.cloned.1.call-done, s32[1024]{0:T(1024)S(1)} %pad_clamp_fusion.1), kind=kCustom, calls=%fused_computation.3 | custom fusion | bytes 11796720 | tf_op jit(solution)/shard_map/gather | solution.py:104
  166.5 15.9 %reshape.243 = bf16[6,1280,3,128]{3,2,1,0:T(4,128)(2,1)} reshape(bf16[60,128,384]{2,1,0:T(8,128)(2,1)} %gather_fusion.3) | data formatting | bytes 11796480 | tf_op jit(solution)/shard_map/reshape | solution.py:104
  182.4 9.4 %fusion.7 = f32[6,3,128,1280]{3,2,1,0:T(8,128)} fusion(bf16[6,1280,3,128]{3,2,1,0:T(4,128)(2,1)} %reshape.243, bf16[6,128,3,42]{3,1,2,0:T(8,128)(2,1)S(1)} %copy.44, bf16[6,128,3,42]{3,1,2,0:T(8,128)(2,1)S(1)} %copy.43, bf16[6,128,3,22]{3,1,2,0:T(8,128)(2,1)S(1)} %copy.42, bf16[6,128,3,22]{3,1,2,0:T(8,128)(2,1)S(1)} %copy.41), kind=kOutput, calls=%fused_computation.13 | convolution fusion | flops 757334016 | bytes 18284544 | tf_op jit(solution)/shard_map/nqhd,nkhd->nhqk/dot_general | solution.py:109
  191.8 15.6 %fusion.37 = (f32[6,3,128]{2,1,0:T(4,128)S(1)}, f32[6,3,128,1280]{3,2,1,0:T(8,128)}) fusion(f32[6,3,128,1280]{3,2,1,0:T(8,128)} %fusion.7), kind=kOutput, calls=%fused_computation.64 | output fusion | flops 11797759 | bytes 23602176 | tf_op jit(solution)/shard_map/sub | solution.py:113
  207.4 28.7 %all-gather.6.cloned.1.call-done = bf16[96,128,384]{2,1,0:T(8,128)(2,1)} async-done(((bf16[6,128,384]{2,1,0:T(8,128)(2,1)}), bf16[96,128,384]{2,1,0:T(8,128)(2,1)}) %all-gather.6.cloned.1.call-update) | async-done | bytes 9437200 | tf_op jit(solution)/shard_map/all_gather | solution.py:102
  236.1 7.8 %gather_fusion = bf16[60,128,384]{2,1,0:T(8,128)(2,1)} fusion(bf16[96,128,384]{2,1,0:T(8,128)(2,1)} %all-gather.6.cloned.1.call-done, s32[1024]{0:T(1024)S(1)} %pad_clamp_fusion.1), kind=kCustom, calls=%fused_computation | custom fusion | bytes 11796720 | tf_op jit(solution)/shard_map/gather | solution.py:105
  243.9 15.8 %reshape.242 = bf16[6,1280,3,128]{3,2,1,0:T(4,128)(2,1)} reshape(bf16[60,128,384]{2,1,0:T(8,128)(2,1)} %gather_fusion) | data formatting | bytes 11796480 | tf_op jit(solution)/shard_map/reshape | solution.py:105
  259.7 9.2 %fusion.19 = bf16[6,128,3,128]{1,3,2,0:T(8,128)(2,1)S(1)} fusion(f32[6,3,128,1280]{3,2,1,0:T(8,128)} %get-tuple-element.24, f32[6,3,128]{2,1,0:T(4,128)S(1)} %get-tuple-element.23, bf16[6,1280,3,128]{3,2,1,0:T(4,128)(2,1)} %reshape.242), kind=kOutput, calls=%fused_computation.21 | convolution fusion | flops 761167872 | bytes 18293760 | tf_op jit(solution)/shard_map/nhqk,nkhd->nqhd/dot_general | solution.py:115
  268.9 0.4 copy.49
  269.3 8.8 %convolution_convert_fusion = bf16[768,5120]{1,0:T(8,128)(2,1)} fusion(bf16[384,5120]{1,0:T(8,128)(2,1)} %param.15, bf16[48,8,6,128]{3,2,1,0:T(8,128)(2,1)S(1)} %bitcast.62), kind=kOutput, calls=%fused_computation.11 | convolution fusion | flops 3023831040 | bytes 12386304 | tf_op jit(solution)/shard_map/dot_general | solution.py:125
  278.1 10.6 %copy.54 = bf16[768,5120]{0,1:T(8,128)(2,1)} copy(bf16[768,5120]{1,0:T(8,128)(2,1)} %convolution_convert_fusion) | data formatting | bytes 15728640
  288.9 0.7 copy-done.6
  289.6 0.9 convolution_convert_fusion.2
  290.5 48.4 %reduce-scatter.4.cloned.1.call-done = bf16[640,768]{1,0:T(8,128)(2,1)} async-done(((bf16[5120,768]{1,0:T(8,128)(2,1)}), bf16[640,768]{1,0:T(8,128)(2,1)}) %reduce-scatter.4.cloned.1.call-update) | async-done | bytes 983056
  338.9 1.5 copy.55
  340.4 58.1 %all-reduce.2.cloned.1.call-done = bf16[768,64]{0,1:T(8,128)(2,1)} async-done(((bf16[768,64]{0,1:T(8,128)(2,1)}), bf16[768,64]{0,1:T(8,128)(2,1)}) %all-reduce.2.cloned.1.call-update) | async-done | bytes 98320 | tf_op jit(solution)/shard_map/psum | solution.py:119
  398.5 2.3 add_convert_fusion
  (33 shorter events, 0.6 us)
Async XLA Ops:
  6.5 52.6 %copy-start = (bf16[5120,192]{0,1:T(8,128)(2,1)S(1)}, bf16[5120,192]{0,1:T(8,128)(2,1)}, u32[]{:S(2)}) copy-start(bf16[5120,192]{0,1:T(8,128)(2,1)} %param.13) | copy-start | bytes 5898244
  6.5 52.6 %all-gather.4.cloned.1.call-start = ((), (), s32[]{:S(2)}) async-start(), calls=%async_computation.1 | async-start | bytes 8847360 | tf_op jit(solution)/shard_map/all_gather | solution.py:72
  7.3 151.5 %all-gather.8.cloned.1.call-start = ((), (), s32[]{:S(2)}) async-start(), calls=%async_computation.3 | async-start | bytes 10027008 | tf_op jit(solution)/shard_map/all_gather | solution.py:101
  27.5 37.8 %copy-start.4 = (bf16[64,3,384]{2,0,1:T(8,128)(2,1)S(1)}, bf16[64,3,384]{2,0,1:T(8,128)(2,1)}, u32[]{:S(2)}) copy-start(bf16[64,3,384]{2,0,1:T(8,128)(2,1)} %param.14) | copy-start | bytes 442372
  59.2 6.8 %copy-start.2 = (bf16[5120,3,384]{0,2,1:T(8,128)(2,1)S(1)}, bf16[5120,3,384]{0,2,1:T(8,128)(2,1)}, u32[]{:S(2)}) copy-start(bf16[5120,3,384]{0,2,1:T(8,128)(2,1)} %copy.37) | copy-start | bytes 35389444
  79.3 1.7 copy-start.3
  79.5 6.4 %copy-start.7 = (s32[96,10]{0,1:T(8,128)S(1)}, s32[96,10]{0,1:T(8,128)}, u32[]{:S(2)}) copy-start(s32[96,10]{0,1:T(8,128)} %param.11) | copy-start | bytes 11524
  83.1 152.9 %all-gather.6.cloned.1.call-start = ((), (), s32[]{:S(2)}) async-start(), calls=%async_computation.2 | async-start | bytes 10027008 | tf_op jit(solution)/shard_map/all_gather | solution.py:102
  85.6 253.2 %reduce-scatter.4.cloned.1.call-start = ((), (), s32[]{:S(2)}) async-start(), calls=%async_computation.5 | async-start | bytes 8847360
  288.8 0.8 copy-start.6
  288.8 109.7 %copy-start.5 = (bf16[64,640]{1,0:T(8,128)(2,1)S(1)}, bf16[64,640]{1,0:T(8,128)(2,1)}, u32[]{:S(2)}) copy-start(bf16[64,640]{1,0:T(8,128)(2,1)} %param.17) | copy-start | bytes 245764
  288.8 112.0 %copy-start.1 = (bf16[5120,192]{0,1:T(8,128)(2,1)S(1)}, bf16[5120,192]{0,1:T(8,128)(2,1)}, u32[]{:S(2)}) copy-start(bf16[5120,192]{0,1:T(8,128)(2,1)} %param.13) | copy-start | bytes 5898244
  288.8 109.7 %all-reduce.2.cloned.1.call-start = ((), (), s32[]{:S(2)}) async-start(), calls=%async_computation.4 | async-start | bytes 196608 | tf_op jit(solution)/shard_map/psum | solution.py:119
Sparse Core Ops, SparseCore 0:
  9.0 50.0 all-gather.3
  83.3 75.4 all-gather.7
  160.9 75.1 all-gather.5
  288.9 49.8 reduce-scatter.3
  341.0 57.4 all-reduce.1
where the time goes:
time: 409 us; the launch traced here: 407 us
  waiting for transfers between devices  238 us (58%)
  local copies, waits for them, and re-layouts  86.9 us (21%)
  matrix products  50.6 us (12%)
  other arithmetic  18.3 us (4%)
  between operations  13.3 us (3%)
    all_gather x1, waiting for transfers between devices, body(): lax.all_gather(key_tiles, 'frame', axis=0, tiled=True)  70.3 us
    psum x1, waiting for transfers between devices, body(): lax.psum(jnp.dot(attention_result, output_down_weight, preferred_element_...  58.1 us
    unnamed x6, waiting for transfers between devices  49.2 us
    all_gather x1, waiting for transfers between devices, body(): rank_segment = lax.all_gather(tokens, 'head', axis=1, tiled=True)  31.6 us
    unnamed x19, local copies, waits for them, and re-layouts  30.2 us
    all_gather x1, waiting for transfers between devices, body(): lax.all_gather(value_tiles, 'frame', axis=0, tiled=True)  28.7 us
    reshape x1, local copies, waits for them, and re-layouts, body(): pool_keys[my_lists]  15.9 us
    reshape x1, local copies, waits for them, and re-layouts, body(): pool_values[my_lists]  15.8 us
  transfers between devices with their start and end apart: 5, of which 5 were waited for; matrix products, arithmetic and copies ran while one was open for 19% of the time, Pallas kernels for 0%

commit v1 on v0

--- a/solution.py
+++ b/solution.py
@@ -7,6 +7,11 @@
 MODEL_WIDTH = 5120
 HEAD_SIZE = 128
 BLOCK = 128
+
+
+def swapped_in(x, axis, along):
+    outgoing = jnp.stack([x] * lax.axis_size(axis))
+    return jnp.concatenate(lax.all_to_all(outgoing, axis, 0, 0), axis=along)
 
 
 def rotate_pairs(values, frame_pos, place):
@@ -69,7 +74,7 @@
     adapter_rank_width = output_up_weight.shape[0]
     listed = attended_key_blocks.shape[1]
     weights_flat = frozen_query_key_value.reshape(MODEL_WIDTH, 3 * local_width)
-    rank_segment = lax.all_gather(tokens, "head", axis=1, tiled=True)
+    rank_segment = swapped_in(tokens, "head", 1)
     projected_rows = jnp.dot(rank_segment, weights_flat, preferred_element_type=jnp.float32)
     adapter_output_sum = jnp.dot(
         rank_segment, query_key_value_down_weight, preferred_element_type=jnp.float32

time: 409 us -> 493 us (1.21); the launches traced: 407 us -> 485 us
  local copies, waits for them, and re-layouts: 86.9 us -> 123 us
  waiting for transfers between devices: 238 us -> 266 us
  starting transfers between devices: 0.35 us -> 15.2 us
    all_to_all x0 -> x1, waiting for transfers between devices: none -> 70.4 us  [swapped_in(): return jnp.concatenate(lax.all_to_all(outgoing, axis, 0, 0), axis=along)]
    all_gather x1 -> x0, waiting for transfers between devices: 31.6 us -> none  [body(): rank_segment = lax.all_gather(tokens, 'head', axis=1, tiled=True)]
    reshape x0 -> x3, local copies, waits for them, and re-layouts: none -> 31.3 us  [swapped_in(): return jnp.concatenate(lax.all_to_all(outgoing, axis, 0, 0), axis=along)]
    all_gather x1, waiting for transfers between devices: 70.3 us -> 60.4 us  [body(): lax.all_gather(key_tiles, 'frame', axis=0, tiled=True)]
    all_gather x1, starting transfers between devices: 0.04 us -> 9.49 us  [body(): lax.all_gather(value_tiles, 'frame', axis=0, tiled=True)]
    all_to_all x0 -> x1, starting transfers between devices: none -> 5.56 us  [swapped_in(): return jnp.concatenate(lax.all_to_all(outgoing, axis, 0, 0), axis=along)]
    another operation x0 -> x1, local copies, waits for them, and re-layouts: none -> 5.15 us  [swapped_in(): outgoing = jnp.stack([x] * lax.axis_size(axis))]
    unnamed x19 -> x27, local copies, waits for them, and re-layouts: 30.2 us -> 28.3 us
  transfers between devices with their start and end apart: 5 -> 5, of which waited for: 5 -> 5; matrix products, arithmetic and copies ran while one was open for 19% -> 15% of each run, Pallas kernels for 0% -> 0%
where the time goes in v1:
time: 493 us; the launch traced here: 485 us
  waiting for transfers between devices  266 us (54%)
  local copies, waits for them, and re-layouts  123 us (25%)
  matrix products  49.4 us (10%)
  other arithmetic  18.2 us (4%)
  starting transfers between devices  15.2 us (3%)
  between operations  13.6 us (3%)
    all_to_all x1, waiting for transfers between devices, swapped_in(): return jnp.concatenate(lax.all_to_all(outgoing, axis, 0, 0), axis=along)  70.4 us
    all_gather x1, waiting for transfers between devices, body(): lax.all_gather(key_tiles, 'frame', axis=0, tiled=True)  60.4 us
    psum x1, waiting for transfers between devices, body(): lax.psum(jnp.dot(attention_result, output_down_weight, preferred_element_...  58.1 us
    unnamed x5, waiting for transfers between devices  48.5 us
    reshape x3, local copies, waits for them, and re-layouts, swapped_in(): return jnp.concatenate(lax.all_to_all(outgoing, axis, 0, 0), axis=along)  31.3 us
    all_gather x1, waiting for transfers between devices, body(): lax.all_gather(value_tiles, 'frame', axis=0, tiled=True)  28.6 us
    unnamed x27, local copies, waits for them, and re-layouts  28.3 us
    reshape x1, local copies, waits for them, and re-layouts, body(): pool_keys[my_lists]  15.9 us
  transfers between devices with their start and end apart: 5, of which 5 were waited for; matrix products, arithmetic and copies ran while one was open for 15% of the time, Pallas kernels for 0%

profile of v1, /device:TPU:0, one launch (start us, length us, event | category | flops | bytes accessed | tf_op | source)
XLA Modules:
  0.0 485.0 jit_solution(13645291746598569102)
XLA Ops:
  6.5 5.2 %stack.2 = bf16[8,768,640]{2,1,0:T(8,128)(2,1)} broadcast(bf16[768,640]{1,0:T(8,128)(2,1)} %param.9), dimensions={1,2} | broadcast | bytes 8847360 | tf_op jit(solution)/shard_map/stack | solution.py:13
  11.7 5.6 %all-to-all-start = ((bf16[8,768,640]{2,1,0:T(8,128)(2,1)}), bf16[8,768,640]{2,1,0:T(8,128)(2,1)}, u32[]{:S(2)}, u32[]{:S(2)}) async-start(bf16[8,768,640]{2,1,0:T(8,128)(2,1)} %stack.2), calls=%async_computation | async-start | bytes 15728640 | tf_op jit(solution)/shard_map/all_to_all | solution.py:14
  17.3 0.6 gather_fusion.1
  18.0 0.2 select_reduce_fusion
  18.2 0.6 gather_fusion.2
  18.8 15.3 %copy.39 = bf16[5120,3,384]{0,2,1:T(8,128)(2,1)} copy(bf16[5120,3,384]{2,0,1:T(8,128)(2,1)} %param.12) | data formatting | bytes 23592960 | tf_op args[3]
  34.3 1.0 multiply_cosine_fusion.1
  35.3 0.6 multiply_cosine_fusion
  35.9 70.4 %all-to-all-done = bf16[8,768,640]{2,1,0:T(8,128)(2,1)} async-done(((bf16[8,768,640]{2,1,0:T(8,128)(2,1)}), bf16[8,768,640]{2,1,0:T(8,128)(2,1)}, u32[]{:S(2)}, u32[]{:S(2)}) %all-to-all-start) | async-done | bytes 7864352 | tf_op jit(solution)/shard_map/all_to_all | solution.py:14
  106.3 10.9 %copy.38 = bf16[768,8,640]{2,1,0:T(8,128)(2,1)} copy(bf16[768,8,640]{2,0,1:T(8,128)(2,1)} %bitcast) | data formatting | bytes 15728640 | tf_op jit(solution)/shard_map/reshape | solution.py:14
  117.2 12.7 %reshape.251 = bf16[768,5120,1]{1,0,2:T(8,128)(2,1)} reshape(bf16[768,8,640]{2,1,0:T(8,128)(2,1)} %copy.38) | data formatting | bytes 15728640 | tf_op jit(solution)/shard_map/reshape | solution.py:14
  129.9 7.8 %copy.58 = bf16[8,96,8,640]{3,2,0,1:T(8,128)(2,1)} copy(bf16[8,96,8,640]{3,2,1,0:T(8,128)(2,1)} %bitcast.17) | data formatting | bytes 15728640 | tf_op jit(solution)/shard_map/reshape | solution.py:14
  137.7 6.1 %convolution_convert_fusion.1 = bf16[768,192]{0,1:T(8,128)(2,1)S(1)} fusion(bf16[768,5120]{1,0:T(8,128)(2,1)} %bitcast.59, bf16[5120,192]{0,1:T(8,128)(2,1)S(1)} %copy-done), kind=kOutput, calls=%fused_computation.21 | convolution fusion | flops 1510096896 | bytes 10125312 | tf_op jit(solution)/shard_map/dot_general | solution.py:79
  143.8 1.6 fusion.35
  145.4 11.2 %bitcast_add_fusion = f32[768,3,384]{0,2,1:T(8,128)} fusion(f32[3,768,384]{1,2,0:T(8,128)S(1)} %fusion.35, bf16[768,5120,1]{1,0,2:T(8,128)(2,1)S(1)} %copy-done.3, bf16[5120,3,384]{0,2,1:T(8,128)(2,1)S(1)} %bitcast.58), kind=kOutput, calls=%fused_computation.17 | convolution fusion | flops 9060581376 | bytes 26738688 | tf_op jit(solution)/shard_map/dot_general | solution.py:78
  156.7 1.8 fusion.33
  158.5 0.3 subtract_convert_fusion.1
  158.9 0.1 subtract_convert_fusion.3
  159.0 0.2 pad_maximum_fusion
  159.2 0.7 convert_element_type.81
  159.9 1.3 copy.47
  161.1 9.5 %all-gather.3.cloned.1.call-start = ((), (), s32[]{:S(2)}) async-start(), calls=%async_computation.2 | async-start | bytes 10027008 | tf_op jit(solution)/shard_map/all_gather | solution.py:107
  170.6 1.4 slice.81
  172.0 1.1 copy.40
  173.4 0.2 concatenate.19
  173.7 0.4 copy.45
  174.1 0.2 concatenate.20
  174.4 0.4 copy.46
  174.9 0.4 copy.43
  175.5 0.4 copy.44
  175.8 60.4 %all-gather.5.cloned.1.call-done = bf16[96,128,384]{2,1,0:T(8,128)(2,1)} async-done(((bf16[6,128,384]{2,1,0:T(8,128)(2,1)}), bf16[96,128,384]{2,1,0:T(8,128)(2,1)}) %all-gather.5.cloned.1.call-update) | async-done | bytes 9437200 | tf_op jit(solution)/shard_map/all_gather | solution.py:106
  236.2 7.8 %gather_fusion.3 = bf16[60,128,384]{2,1,0:T(8,128)(2,1)} fusion(bf16[96,128,384]{2,1,0:T(8,128)(2,1)} %all-gather.5.cloned.1.call-done, s32[1024]{0:T(1024)S(1)} %pad_clamp_fusion.1), kind=kCustom, calls=%fused_computation.3 | custom fusion | bytes 11796720 | tf_op jit(solution)/shard_map/gather | solution.py:109
  244.0 15.9 %reshape.254 = bf16[6,1280,3,128]{3,2,1,0:T(4,128)(2,1)} reshape(bf16[60,128,384]{2,1,0:T(8,128)(2,1)} %gather_fusion.3) | data formatting | bytes 11796480 | tf_op jit(solution)/shard_map/reshape | solution.py:109
  259.9 9.4 %fusion.6 = f32[6,3,128,1280]{3,2,1,0:T(8,128)} fusion(bf16[6,1280,3,128]{3,2,1,0:T(4,128)(2,1)} %reshape.254, bf16[6,128,3,42]{3,1,2,0:T(8,128)(2,1)S(1)} %copy.46, bf16[6,128,3,42]{3,1,2,0:T(8,128)(2,1)S(1)} %copy.45, bf16[6,128,3,22]{3,1,2,0:T(8,128)(2,1)S(1)} %copy.44, bf16[6,128,3,22]{3,1,2,0:T(8,128)(2,1)S(1)} %copy.43), kind=kOutput, calls=%fused_computation.12 | convolution fusion | flops 757334016 | bytes 18284544 | tf_op jit(solution)/shard_map/nqhd,nkhd->nhqk/dot_general | solution.py:114
  269.3 15.6 %fusion.34 = (f32[6,3,128]{2,1,0:T(4,128)S(1)}, f32[6,3,128,1280]{3,2,1,0:T(8,128)}) fusion(f32[6,3,128,1280]{3,2,1,0:T(8,128)} %fusion.6), kind=kOutput, calls=%fused_computation.63 | output fusion | flops 11797759 | bytes 23602176 | tf_op jit(solution)/shard_map/sub | solution.py:118
  284.9 28.6 %all-gather.3.cloned.1.call-done = bf16[96,128,384]{2,1,0:T(8,128)(2,1)} async-done(((bf16[6,128,384]{2,1,0:T(8,128)(2,1)}), bf16[96,128,384]{2,1,0:T(8,128)(2,1)}) %all-gather.3.cloned.1.call-update) | async-done | bytes 9437200 | tf_op jit(solution)/shard_map/all_gather | solution.py:107
  313.5 7.8 %gather_fusion = bf16[60,128,384]{2,1,0:T(8,128)(2,1)} fusion(bf16[96,128,384]{2,1,0:T(8,128)(2,1)} %all-gather.3.cloned.1.call-done, s32[1024]{0:T(1024)S(1)} %pad_clamp_fusion.1), kind=kCustom, calls=%fused_computation | custom fusion | bytes 11796720 | tf_op jit(solution)/shard_map/gather | solution.py:110
  321.3 15.8 %reshape.253 = bf16[6,1280,3,128]{3,2,1,0:T(4,128)(2,1)} reshape(bf16[60,128,384]{2,1,0:T(8,128)(2,1)} %gather_fusion) | data formatting | bytes 11796480 | tf_op jit(solution)/shard_map/reshape | solution.py:110
  337.2 9.2 %fusion.16 = bf16[6,128,3,128]{1,3,2,0:T(8,128)(2,1)S(1)} fusion(f32[6,3,128,1280]{3,2,1,0:T(8,128)} %get-tuple-element.24, f32[6,3,128]{2,1,0:T(4,128)S(1)} %get-tuple-element.23, bf16[6,1280,3,128]{3,2,1,0:T(4,128)(2,1)} %reshape.253), kind=kOutput, calls=%fused_computation.20 | convolution fusion | flops 761167872 | bytes 18293760 | tf_op jit(solution)/shard_map/nhqk,nkhd->nqhd/dot_general | solution.py:120
  346.4 0.4 copy.51
  346.8 8.8 %convolution_convert_fusion = bf16[768,5120]{1,0:T(8,128)(2,1)} fusion(bf16[384,5120]{1,0:T(8,128)(2,1)} %param.15, bf16[48,8,6,128]{3,2,1,0:T(8,128)(2,1)S(1)} %bitcast.64), kind=kOutput, calls=%fused_computation.11 | convolution fusion | flops 3023831040 | bytes 12386304 | tf_op jit(solution)/shard_map/dot_general | solution.py:130
  355.5 10.6 %copy.56 = bf16[768,5120]{0,1:T(8,128)(2,1)} copy(bf16[768,5120]{1,0:T(8,128)(2,1)} %convolution_convert_fusion) | data formatting | bytes 15728640
  366.2 0.7 copy-done.7
  367.0 0.9 convolution_convert_fusion.2
  367.8 48.4 %reduce-scatter.4.cloned.1.call-done = bf16[640,768]{1,0:T(8,128)(2,1)} async-done(((bf16[5120,768]{1,0:T(8,128)(2,1)}), bf16[640,768]{1,0:T(8,128)(2,1)}) %reduce-scatter.4.cloned.1.call-update) | async-done | bytes 983056
  416.2 1.5 copy.57
  417.8 58.1 %all-reduce.2.cloned.1.call-done = bf16[768,64]{0,1:T(8,128)(2,1)} async-done(((bf16[768,64]{0,1:T(8,128)(2,1)}), bf16[768,64]{0,1:T(8,128)(2,1)}) %all-reduce.2.cloned.1.call-update) | async-done | bytes 98320 | tf_op jit(solution)/shard_map/psum | solution.py:124
  475.9 2.3 add_convert_fusion
  (45 shorter events, 0.9 us)
Async XLA Ops:
  6.5 131.2 %copy-start = (bf16[5120,192]{0,1:T(8,128)(2,1)S(1)}, bf16[5120,192]{0,1:T(8,128)(2,1)}, u32[]{:S(2)}) copy-start(bf16[5120,192]{0,1:T(8,128)(2,1)} %param.13) | copy-start | bytes 5898244
  11.7 5.6 %copy-start.2 = (s32[96]{0:T(128)S(1)}, s32[96]{0:T(128)}, u32[]{:S(2)}) copy-start(s32[96]{0:T(128)} %param.10) | copy-start | bytes 1156
  11.7 94.6 %all-to-all-start = ((bf16[8,768,640]{2,1,0:T(8,128)(2,1)}), bf16[8,768,640]{2,1,0:T(8,128)(2,1)}, u32[]{:S(2)}, u32[]{:S(2)}) async-start(bf16[8,768,640]{2,1,0:T(8,128)(2,1)} %stack.2), calls=%async_computation | async-start | bytes 15728640 | tf_op jit(solution)/shard_map/all_to_all | solution.py:14
  17.3 219.0 %all-gather.5.cloned.1.call-start = ((), (), s32[]{:S(2)}) async-start(), calls=%async_computation.3 | async-start | bytes 10027008 | tf_op jit(solution)/shard_map/all_gather | solution.py:106
  129.9 15.5 %slice-start = ((s8[11796480]{0:T(1024)(128)(4,1)}), s8[3407872]{0:T(1024)(128)(4,1)S(1)}, s32[]{:S(2)}) async-start(s8[11796480]{0:T(1024)(128)(4,1)} %bitcast.57), calls=%async_computation.6 | async-start | bytes 6815744
  129.9 15.5 %slice-start.1 = ((s8[11796480]{0:T(1024)(128)(4,1)}), s8[4194304]{0:T(1024)(128)(4,1)S(1)}, s32[]{:S(2)}) async-start(s8[11796480]{0:T(1024)(128)(4,1)} %bitcast.57), calls=%async_computation.7 | async-start | bytes 8388608
  137.7 7.7 %slice-start.2 = ((s8[11796480]{0:T(1024)(128)(4,1)}), s8[4194304]{0:T(1024)(128)(4,1)S(1)}, s32[]{:S(2)}) async-start(s8[11796480]{0:T(1024)(128)(4,1)} %bitcast.57), calls=%async_computation.8 | async-start | bytes 8388608
  137.7 7.7 %copy-start.3 = (bf16[768,5120,1]{1,0,2:T(8,128)(2,1)S(1)}, bf16[768,5120,1]{1,0,2:T(8,128)(2,1)}, u32[]{:S(2)}) copy-start(bf16[768,5120,1]{1,0,2:T(8,128)(2,1)} %reshape.251) | copy-start | bytes 23592964
  156.7 2.2 copy-start.4
  156.7 2.2 copy-start.5
  158.5 14.7 %copy-start.8 = (s32[96,10]{0,1:T(8,128)S(1)}, s32[96,10]{0,1:T(8,128)}, u32[]{:S(2)}) copy-start(s32[96,10]{0,1:T(8,128)} %param.11) | copy-start | bytes 11524
  161.1 152.4 %all-gather.3.cloned.1.call-start = ((), (), s32[]{:S(2)}) async-start(), calls=%async_computation.2 | async-start | bytes 10027008 | tf_op jit(solution)/shard_map/all_gather | solution.py:107
  173.1 243.1 %reduce-scatter.4.cloned.1.call-start = ((), (), s32[]{:S(2)}) async-start(), calls=%async_computation.5 | async-start | bytes 8847360
  366.2 0.8 copy-start.7
  366.2 109.7 %copy-start.6 = (bf16[64,640]{1,0:T(8,128)(2,1)S(1)}, bf16[64,640]{1,0:T(8,128)(2,1)}, u32[]{:S(2)}) copy-start(bf16[64,640]{1,0:T(8,128)(2,1)} %param.17) | copy-start | bytes 245764
  366.2 112.0 %copy-start.1 = (bf16[5120,192]{0,1:T(8,128)(2,1)S(1)}, bf16[5120,192]{0,1:T(8,128)(2,1)}, u32[]{:S(2)}) copy-start(bf16[5120,192]{0,1:T(8,128)(2,1)} %param.13) | copy-start | bytes 5898244
  366.2 109.7 %all-reduce.2.cloned.1.call-start = ((), (), s32[]{:S(2)}) async-start(), calls=%async_computation.4 | async-start | bytes 196608 | tf_op jit(solution)/shard_map/psum | solution.py:124
Sparse Core Ops, SparseCore 0:
  161.3 74.9 all-gather.4
  238.4 75.1 all-gather.2
  366.3 49.8 reduce-scatter.3
  418.4 57.4 all-reduce.1
